TPU v7x, 128 devices: a whole 4x4x4 slice. The times are simulated.
128 devices in a mesh: rep: 16 (over y_lo, z, core), shard: 8 (over x, y_hi).
Axes of the slice: x: 4, y: 4 (y_hi: 2, y_lo: 2; y = y_hi * 2 + y_lo), z: 4, core: 2. Of those that a mesh axis runs over, the one named last changes fastest.
Arguments:
- hidden_in: float32 [16384, 1024], P(('rep', 'shard')), may hold values from -6 to 6
- doc_start: int32 [16384], P(('rep', 'shard')), may hold values from 0 to 127, as said below
- grad_out: float32 [16384, 1024], P(('rep', 'shard')), may hold values from -6 to 6
- w_qkv: bfloat16 [2, 1024, 3072], P(None, 'shard'), may hold values from -0.1875 to 0.1875
- w_proj: bfloat16 [2, 1024, 1024], P(None, 'shard'), may hold values from -0.375 to 0.375
- w_up: bfloat16 [2, 1024, 4096], P(None, 'shard'), may hold values from -0.1875 to 0.1875
- w_down: bfloat16 [2, 4096, 1024], P(None, 'shard'), may hold values from -0.09375 to 0.09375
- norm_gain: bfloat16 [2, 1024, 2], P(None, 'shard'), may hold values from 0.5 to 1.5
- d_bias: bfloat16 [2, 1024, 6], P(None, 'shard'), may hold values from -3 to 3
- up_bias: bfloat16 [2, 4096], P(None, 'shard'), may hold values from -3 to 3
Outputs:
- hidden_out: float32 [16384, 1024], P(('rep', 'shard'))
- grad_in: float32 [16384, 1024], P(('rep', 'shard'))
- grad_qkv: float32 [2, 1024, 3072], P(None, 'shard')
- grad_proj: float32 [2, 1024, 1024], P(None, 'shard')
- grad_up: float32 [2, 1024, 4096], P(None, 'shard')
- grad_down: float32 [2, 4096, 1024], P(None, 'shard')
- grad_gain: float32 [2, 1024, 2], P(None, 'shard')
- grad_dbias: float32 [2, 1024, 6], P(None, 'shard')
- grad_upbias: float32 [2, 4096], P(None, 'shard')
Inputs may be any that keep to these rules, and one draw needn't show every extreme that they name: `doc_start`: each aligned run of 128 slots holds whole documents in order: the value does not fall along a run, is 0 at the run's first slot, and equals the slot's own offset at a document's first token.
All inputs are finite; a program needn't handle non-finite values.
Results may differ from a plain program's by a relative error of at most 0.025.
Values may be sent and summed in bfloat16 or wider, within the bound.
No kernel may reach another device: no remote copies, remote signals or barrier semaphores. Data moves between devices by JAX's collectives and lax.ppermute only.
A program may use at most 256 MiB of HBM per device.

v0:
```python
import jax
import jax.numpy as jnp
from jax import lax
from jax.sharding import PartitionSpec as P

HEADS = 16
HEAD_DIM = 64
LAYERS = 2
epsilon = 1e-05
gelu_coef = 0.7978845608


def in_one_piece(arrays, axis, dim, along):
    both = jnp.concatenate(arrays, axis=along)
    result, at, done = (lax.all_gather(both, axis, axis=dim, tiled=True), 0, [])
    for a in arrays:
        done.append(lax.slice_in_dim(result, at, at + a.shape[along], axis=along))
        at += a.shape[along]
    return tuple(done)


def split_up(shard, dim, length):
    shape = shard.shape
    tiles = shard.reshape(*shape[:dim], length, shape[dim] // length, *shape[dim + 1 :])
    return jnp.moveaxis(tiles, dim, 0)


def sent_and_summed(shard, axis, dim):
    length = lax.axis_size(axis)
    tiles = lax.all_to_all(split_up(shard, dim, length), axis, 0, 0, tiled=True)
    return jnp.sum(tiles.astype(jnp.float32), axis=0)


def sent_together(arrays, axis, dim, along):
    both = jnp.concatenate(arrays, axis=along)
    result, at, done = (sent_and_summed(both, axis, dim), 0, [])
    for a in arrays:
        done.append(lax.slice_in_dim(result, at, at + a.shape[along], axis=along))
        at += a.shape[along]
    return tuple(done)


def batch_prod(form, left, right):
    return jnp.einsum(form, left, right, preferred_element_type=jnp.float32)


def layer_norm(stream, gains, shifts):
    average = jnp.mean(stream, axis=-1, keepdims=True)
    centered = stream - average
    variance = jnp.mean(centered * centered, axis=-1, keepdims=True)
    inv_std = lax.rsqrt(variance + epsilon)
    normed = centered * inv_std
    return (normed * gains + shifts, normed, inv_std)


def norm_back(grad_norm, normed, inv_std, gains):
    scaled = grad_norm * gains
    inner = (
        scaled
        - jnp.mean(scaled, axis=-1, keepdims=True)
        - normed * jnp.mean(scaled * normed, axis=-1, keepdims=True)
    )
    return (inv_std * inner, jnp.sum(grad_norm * normed, axis=0), jnp.sum(grad_norm, axis=0))


def gelu_tanh(values):
    inner = jnp.tanh(gelu_coef * (values + 0.044715 * values * values * values))
    return 0.5 * values * (1.0 + inner)


def gelu_slope(values):
    inner = jnp.tanh(gelu_coef * (values + 0.044715 * values * values * values))
    return 0.5 * (1.0 + inner) + 0.5 * values * (1.0 - inner * inner) * gelu_coef * (
        1.0 + 3.0 * 0.044715 * values * values
    )


def scores_of(query, keys_bf, starts):
    count = query.shape[0]
    query_heads = query.reshape(count, HEADS, HEAD_DIM)
    key_heads = keys_bf.reshape(count, HEADS, HEAD_DIM)
    scores = batch_prod("qhd,khd->hqk", query_heads, key_heads) * HEAD_DIM ** (-0.5)
    offsets = jnp.arange(count, dtype=jnp.int32)
    distance = (offsets[:, None] - offsets[None, :]).astype(jnp.float32)
    head_ids = jnp.arange(HEADS, dtype=jnp.int32).astype(jnp.float32)
    slopes = 2.0 ** (-8.0 * (head_ids + 1.0) / HEADS)
    scores = scores - slopes[:, None, None] * distance[None, :, :]
    visible = (starts[:, None] == starts[None, :]) & (offsets[None, :] <= offsets[:, None])
    return jnp.where(visible[None, :, :], scores, jnp.float32(-1000000000.0))


def layer_forward(stream, starts, wqkv, wproj, wupper, wlower, gains, biases, ubias):
    count, width = stream.shape
    gains = gains.astype(jnp.float32)
    biases = biases.astype(jnp.float32)
    first_f, normed_one, inv_one = layer_norm(stream, gains[:, 0], biases[:, 0])
    first_in = first_f.astype(jnp.bfloat16)
    merged = jnp.dot(first_in, wqkv, preferred_element_type=jnp.float32)
    query = (merged[:, :width] + biases[:, 2]).astype(jnp.bfloat16)
    keys_bf = merged[:, width : 2 * width].astype(jnp.bfloat16)
    values_bf = (merged[:, 2 * width :] + biases[:, 3]).astype(jnp.bfloat16)
    scores = scores_of(query, keys_bf, starts)
    top_score = jnp.max(scores, axis=-1, keepdims=True)
    log_total = top_score + jnp.log(jnp.sum(jnp.exp(scores - top_score), axis=-1, keepdims=True))
    weights_bf = jnp.exp(scores - log_total).astype(jnp.bfloat16)
    context = batch_prod("hqk,khd->qhd", weights_bf, values_bf.reshape(count, HEADS, HEAD_DIM))
    context = context.reshape(count, width).astype(jnp.bfloat16)
    middle = stream + jnp.dot(context, wproj, preferred_element_type=jnp.float32) + biases[:, 4]
    second_f, normed_two, inv_two = layer_norm(middle, gains[:, 1], biases[:, 1])
    second_in = second_f.astype(jnp.bfloat16)
    upper = jnp.dot(second_in, wupper, preferred_element_type=jnp.float32) + ubias.astype(
        jnp.float32
    )
    activ = gelu_tanh(upper).astype(jnp.bfloat16)
    result = middle + jnp.dot(activ, wlower, preferred_element_type=jnp.float32) + biases[:, 5]
    kept = (
        first_in,
        normed_one,
        inv_one,
        query,
        keys_bf,
        values_bf,
        log_total,
        context,
        second_in,
        normed_two,
        inv_two,
        upper,
        activ,
    )
    return (result, kept)


def layer_backward(
    grad_y, starts, kept, wqkv, wproj, wupper, wlower, gains, biases, ubias, full_terms
):
    (
        first_in,
        normed_one,
        inv_one,
        query,
        keys_bf,
        values_bf,
        log_total,
        context,
        second_in,
        normed_two,
        inv_two,
        upper,
        activ,
    ) = kept
    count, width = grad_y.shape
    gains = gains.astype(jnp.float32)
    grad_yb = grad_y.astype(jnp.bfloat16)
    g_bdown = jnp.sum(grad_y, axis=0)
    grad_act = jnp.dot(grad_yb, wlower.T, preferred_element_type=jnp.float32)
    grad_upper = grad_act * gelu_slope(upper)
    g_ubias = jnp.sum(grad_upper, axis=0)
    grad_ub = grad_upper.astype(jnp.bfloat16)
    grad_two = jnp.dot(grad_ub, wupper.T, preferred_element_type=jnp.float32)
    back_two, g_gain_two, g_shift_two = norm_back(grad_two, normed_two, inv_two, gains[:, 1])
    grad_mid = grad_y + back_two
    grad_midb = grad_mid.astype(jnp.bfloat16)
    g_bproj = jnp.sum(grad_mid, axis=0)
    grad_ctx = jnp.dot(grad_midb, wproj.T, preferred_element_type=jnp.float32).astype(jnp.bfloat16)
    scores = scores_of(query, keys_bf, starts)
    probs = jnp.exp(scores - log_total)
    probs_bf = probs.astype(jnp.bfloat16)
    ctx_heads = grad_ctx.reshape(count, HEADS, HEAD_DIM)
    grad_val = batch_prod("hqk,qhd->khd", probs_bf, ctx_heads)
    grad_prob = batch_prod("qhd,khd->hqk", ctx_heads, values_bf.reshape(count, HEADS, HEAD_DIM))
    delta = jnp.sum(
        ctx_heads.astype(jnp.float32) * context.reshape(count, HEADS, HEAD_DIM).astype(jnp.float32),
        axis=-1,
    )
    grad_score = (probs * (grad_prob - jnp.transpose(delta)[:, :, None])).astype(jnp.bfloat16)
    grad_query = batch_prod(
        "hqk,khd->qhd", grad_score, keys_bf.reshape(count, HEADS, HEAD_DIM)
    ) * HEAD_DIM ** (-0.5)
    grad_key = batch_prod(
        "hqk,qhd->khd", grad_score, query.reshape(count, HEADS, HEAD_DIM)
    ) * HEAD_DIM ** (-0.5)
    grad_query = grad_query.reshape(count, width)
    grad_key = grad_key.reshape(count, width)
    grad_val = grad_val.reshape(count, width)
    g_bquery = jnp.sum(grad_query, axis=0)
    g_bvalue = jnp.sum(grad_val, axis=0)
    grad_merged = jnp.concatenate([grad_query, grad_key, grad_val], axis=1).astype(jnp.bfloat16)
    grad_one = jnp.dot(grad_merged, wqkv.T, preferred_element_type=jnp.float32)
    back_one, g_gain_one, g_shift_one = norm_back(grad_one, normed_one, inv_one, gains[:, 0])
    grad_x = grad_mid + back_one
    g_gain = jnp.stack([g_gain_one, g_gain_two], axis=1)
    g_bias = jnp.stack([g_shift_one, g_shift_two, g_bquery, g_bvalue, g_bproj, g_bdown], axis=1)
    g_down, g_up, g_proj, g_qkv = (None, None, None, None)
    operands = (grad_yb, grad_ub, grad_midb, grad_merged)
    return (grad_x, (g_qkv, g_proj, g_up, g_down, g_gain, g_bias, g_ubias), operands)


def local(hidden_in, doc_start, grad_out, w_qkv, w_proj, w_up, w_down, norm_gain, d_bias, up_bias):
    saved = []
    current = hidden_in
    for layer_no in range(LAYERS):
        whole = (
            *in_one_piece((w_qkv[layer_no], w_proj[layer_no], w_up[layer_no]), "shard", 0, 1),
            lax.all_gather(w_down[layer_no], "shard", axis=0, tiled=True),
            *in_one_piece((norm_gain[layer_no], d_bias[layer_no]), "shard", 0, 1),
            lax.all_gather(up_bias[layer_no], "shard", axis=0, tiled=True),
        )
        current, kept = layer_forward(current, doc_start, *whole)
        saved.append(kept)
    running = grad_out
    owned = [None] * LAYERS
    for layer_no in reversed(range(LAYERS)):
        whole = (
            *in_one_piece((w_qkv[layer_no], w_proj[layer_no], w_up[layer_no]), "shard", 0, 1),
            lax.all_gather(w_down[layer_no], "shard", axis=0, tiled=True),
            *in_one_piece((norm_gain[layer_no], d_bias[layer_no]), "shard", 0, 1),
            lax.all_gather(up_bias[layer_no], "shard", axis=0, tiled=True),
        )
        kept = saved[layer_no]
        running, terms, operands = layer_backward(running, doc_start, kept, *whole, False)
        joined = in_one_piece((operands[0], operands[1], operands[2], operands[3]), "shard", 0, 1)
        pieces = (
            lax.all_to_all(kept[0], "shard", split_axis=1, concat_axis=0, tiled=True),
            lax.all_to_all(kept[7], "shard", split_axis=1, concat_axis=0, tiled=True),
            lax.all_to_all(kept[8], "shard", split_axis=1, concat_axis=0, tiled=True),
            lax.all_to_all(kept[12], "shard", split_axis=1, concat_axis=0, tiled=True),
        )
        own_qkv = jnp.dot(pieces[0].T, joined[3], preferred_element_type=jnp.float32)
        own_proj = jnp.dot(pieces[1].T, joined[2], preferred_element_type=jnp.float32)
        own_up = jnp.dot(pieces[2].T, joined[1], preferred_element_type=jnp.float32)
        own_down = jnp.dot(pieces[3].T, joined[0], preferred_element_type=jnp.float32)
        small = (
            *sent_together(
                (terms[4].astype(jnp.bfloat16), terms[5].astype(jnp.bfloat16)), "shard", 0, 1
            ),
            sent_and_summed(terms[6].astype(jnp.bfloat16), "shard", 0),
        )
        shares = (own_qkv, own_proj, own_up, own_down, small[0], small[1], small[2])
        shares = (
            lax.psum(shares[0].astype(jnp.bfloat16), "rep").astype(jnp.float32),
            lax.psum(shares[1].astype(jnp.bfloat16), "rep").astype(jnp.float32),
            lax.psum(shares[2].astype(jnp.bfloat16), "rep").astype(jnp.float32),
            lax.psum(shares[3].astype(jnp.bfloat16), "rep").astype(jnp.float32),
            lax.psum(shares[4].astype(jnp.bfloat16), "rep").astype(jnp.float32),
            lax.psum(shares[5].astype(jnp.bfloat16), "rep").astype(jnp.float32),
            lax.psum(shares[6].astype(jnp.bfloat16), "rep").astype(jnp.float32),
        )
        owned[layer_no] = shares
    stacked = [
        jnp.stack([owned[layer_no][slot] for layer_no in range(LAYERS)]) for slot in range(7)
    ]
    return (
        current,
        running,
        stacked[0],
        stacked[1],
        stacked[2],
        stacked[3],
        stacked[4],
        stacked[5],
        stacked[6],
    )


def solution(mesh):
    placed = (
        P(("rep", "shard"), None),
        P(("rep", "shard")),
        P(("rep", "shard"), None),
        P(None, "shard", None),
        P(None, "shard", None),
        P(None, "shard", None),
        P(None, "shard", None),
        P(None, "shard", None),
        P(None, "shard", None),
        P(None, "shard"),
    )
    return jax.shard_map(
        local,
        mesh=mesh,
        in_specs=placed,
        out_specs=(
            P(("rep", "shard"), None),
            P(("rep", "shard"), None),
            P(None, "shard", None),
            P(None, "shard", None),
            P(None, "shard", None),
            P(None, "shard", None),
            P(None, "shard", None),
            P(None, "shard", None),
            P(None, "shard"),
        ),
        check_vma=False,
    )
```

profile of v0, /device:TPU:0, one launch (start us, length us, event | category | flops | bytes accessed | tf_op | source)
XLA Modules:
  0.0 1301.5 jit_solution(16757099356191935756)
XLA Ops:
  17.2 30.1 %all-gather = bf16[1,4096]{1,0:T(2,128)(2,1)S(1)} all-gather(bf16[1,512]{1,0:T(2,128)(2,1)S(1)} %get-tuple-element.107), channel_id=2, replica_groups=mesh['rep'=16,'shard'=8] {'shard'}, dimensions={1}, use_global_device_ids=true | all-gather | bytes 9216 | tf_op jit(solution)/shard_map/all_gather | solution.py:207
  47.4 29.7 %all-gather.2 = bf16[1,4096]{1,0:T(2,128)(2,1)S(1)} all-gather(bf16[1,512]{1,0:T(2,128)(2,1)S(1)} %get-tuple-element.106), channel_id=4, replica_groups=mesh['rep'=16,'shard'=8] {'shard'}, dimensions={1}, use_global_device_ids=true | all-gather | bytes 9216 | tf_op jit(solution)/shard_map/all_gather | solution.py:207
  77.2 29.7 %all_gather.36 = bf16[1024,8]{0,1:T(8,128)(2,1)S(1)} all-gather(bf16[128,8]{0,1:T(8,128)(2,1)S(1)} %pad_maximum_fusion.2), channel_id=1, replica_groups=mesh['rep'=16,'shard'=8] {'shard'}, dimensions={0}, use_global_device_ids=true | all-gather | bytes 18432 | tf_op jit(solution)/shard_map/all_gather | solution.py:15
  107.0 29.8 %all_gather.40 = bf16[1024,8]{0,1:T(8,128)(2,1)S(1)} all-gather(bf16[128,8]{0,1:T(8,128)(2,1)S(1)} %pad_maximum_fusion.3), channel_id=1, replica_groups=mesh['rep'=16,'shard'=8] {'shard'}, dimensions={0}, use_global_device_ids=true | all-gather | bytes 18432 | tf_op jit(solution)/shard_map/all_gather | solution.py:15
  138.0 63.1 %all-gather.11.cloned.1.call-done = bf16[1024,8192]{1,0:T(8,128)(2,1)} async-done(((bf16[128,8192]{1,0:T(8,128)(2,1)}), bf16[1024,8192]{1,0:T(8,128)(2,1)}) %all-gather.11.cloned.1.call-update) | async-done | bytes 16777232 | tf_op jit(solution)/shard_map/all_gather | solution.py:15
  209.0 7.7 multiply_convert_fusion.1
  216.7 93.6 %all-gather.19.cloned.1.call-done = bf16[1,4096,1024]{2,1,0:T(8,128)(2,1)} async-done(((bf16[1,512,1024]{2,1,0:T(8,128)(2,1)}), bf16[1,4096,1024]{2,1,0:T(8,128)(2,1)}) %all-gather.19.cloned.1.call-update) | async-done | bytes 8388624 | tf_op jit(solution)/shard_map/all_gather | solution.py:205
  315.6 181.5 %all-gather.13.cloned.1.call-done = bf16[1024,8192]{1,0:T(8,128)(2,1)} async-done(((bf16[128,8192]{1,0:T(8,128)(2,1)}), bf16[1024,8192]{1,0:T(8,128)(2,1)}) %all-gather.13.cloned.1.call-update) | async-done | bytes 16777232 | tf_op jit(solution)/shard_map/all_gather | solution.py:15
  506.8 7.7 multiply_convert_fusion
  514.4 91.6 %all-gather.21.cloned.1.call-done = bf16[1,4096,1024]{2,1,0:T(8,128)(2,1)} async-done(((bf16[1,512,1024]{2,1,0:T(8,128)(2,1)}), bf16[1,4096,1024]{2,1,0:T(8,128)(2,1)}) %all-gather.21.cloned.1.call-update) | async-done | bytes 8388624 | tf_op jit(solution)/shard_map/all_gather | solution.py:205
  606.1 8.7 convert_dynamic-update-slice_fusion.1
  614.8 7.0 fusion.12
  643.5 8.1 fusion.16
  674.5 8.5 all-to-all-done.4
  716.0 168.9 %all-gather.15.cloned.1.call-done = bf16[1024,9216]{1,0:T(8,128)(2,1)} async-done(((bf16[128,9216]{1,0:T(8,128)(2,1)}), bf16[1024,9216]{1,0:T(8,128)(2,1)}) %all-gather.15.cloned.1.call-update) | async-done | bytes 18874384 | tf_op jit(solution)/shard_map/all_gather | solution.py:15
  889.7 5.6 fusion.53
  903.9 198.0 %all-gather.17.cloned.1.call-done = bf16[1024,9216]{1,0:T(8,128)(2,1)} async-done(((bf16[128,9216]{1,0:T(8,128)(2,1)}), bf16[1024,9216]{1,0:T(8,128)(2,1)}) %all-gather.17.cloned.1.call-update) | async-done | bytes 18874384 | tf_op jit(solution)/shard_map/all_gather | solution.py:15
  1101.9 5.7 fusion.50
  1164.8 7.1 all-to-all-start.11
  1172.5 7.1 all-to-all-done.11
  1183.6 7.0 all-to-all-done.8
  1195.1 6.4 all-to-all-done.9
  1201.6 28.4 %all-reduce = (bf16[1,128,2]{1,2,0:T(2,128)(2,1)S(1)}, bf16[1,128,2]{1,2,0:T(2,128)(2,1)S(1)}, bf16[1,128,6]{1,2,0:T(8,128)(2,1)S(1)}, bf16[1,128,6]{1,2,0:T(8,1...) all-reduce(bf16[1,128,2]{1,2,0:T(2,128)(2,1)S(1)} %slice_bitcast_fu, ...), channel_id=1, replica_groups=mesh['rep'=16,'shard'=8] {'rep'}, use_global_device_ids=true, to_apply=%region_49.50 | all-reduce | flops 3072 | bytes 12288 | tf_op jit(solution)/shard_map/psum | solution.py:245
  1231.8 52.5 %all-reduce.4.cloned.1.call-done = (bf16[1,128,3072]{2,1,0:T(8,128)(2,1)}, bf16[1,128,3072]{2,1,0:T(8,128)(2,1)}, bf16[1,128,1024]{2,1,0:T(8,128)(2,1)}, bf16[1,...) async-done(((bf16[1,128,3072]{2,1,0:T(8,128)(2,1)}, ...) | async-done | bytes 6291472 | tf_op jit(solution)/shard_map/psum | solution.py:241
  (368 shorter events, 201.9 us)
Async XLA Ops:
  7.2 194.0 %all-gather.11.cloned.1.call-start = ((), (), s32[]{:S(2)}) async-start(), calls=%async_computation.12 | async-start | bytes 18874368 | tf_op jit(solution)/shard_map/all_gather | solution.py:15
  11.8 298.5 %all-gather.19.cloned.1.call-start = ((), (), s32[]{:S(2)}) async-start(), calls=%async_computation.16 | async-start | bytes 9437184 | tf_op jit(solution)/shard_map/all_gather | solution.py:205
  15.0 482.1 %all-gather.13.cloned.1.call-start = ((), (), s32[]{:S(2)}) async-start(), calls=%async_computation.13 | async-start | bytes 18874368 | tf_op jit(solution)/shard_map/all_gather | solution.py:15
  16.5 120.6 %copy-start.69 = (s32[128]{0:T(128)S(1)}, s32[128]{0:T(128)}, u32[]{:S(2)}) copy-start(s32[128]{0:T(128)} %param.11) | copy-start | bytes 1540
  16.5 120.8 %copy-start.21 = (f32[128,1024]{1,0:T(8,128)S(1)}, f32[128,1024]{1,0:T(8,128)}, u32[]{:S(2)}) copy-start(f32[128,1024]{1,0:T(8,128)} %param.12) | copy-start | bytes 1572868
  16.5 589.5 %all-gather.21.cloned.1.call-start = ((), (), s32[]{:S(2)}) async-start(), calls=%async_computation.17 | async-start | bytes 9437184 | tf_op jit(solution)/shard_map/all_gather | solution.py:205
  17.1 867.7 %all-gather.15.cloned.1.call-start = ((), (), s32[]{:S(2)}) async-start(), calls=%async_computation.14 | async-start | bytes 21233664 | tf_op jit(solution)/shard_map/all_gather | solution.py:15
  315.3 185.6 %copy-start.3 = (f32[128,1024]{1,0:T(8,128)}, f32[128,1024]{1,0:T(8,128)S(1)}, u32[]{:S(2)}) copy-start(f32[128,1024]{1,0:T(8,128)S(1)} %get-tuple-element.117) | copy-start | bytes 1572868
  315.4 185.6 %copy-start.65 = (f32[128]{0:T(128)}, f32[128]{0:T(128)S(1)}, u32[]{:S(2)}) copy-start(f32[128]{0:T(128)S(1)} %broadcast_multiply_fusion.9) | copy-start | bytes 1540
  315.6 185.3 %copy-start.72 = (f32[128]{0:T(128)}, f32[128]{0:T(128)S(1)}, u32[]{:S(2)}) copy-start(f32[128]{0:T(128)S(1)} %add_rsqrt_fusion.1) | copy-start | bytes 1540
  665.6 436.3 %all-gather.17.cloned.1.call-start = ((), (), s32[]{:S(2)}) async-start(), calls=%async_computation.15 | async-start | bytes 21233664 | tf_op jit(solution)/shard_map/all_gather | solution.py:15
  670.3 12.7 all-to-all-start.4
  683.0 14.2 %all-to-all-start.5 = ((bf16[128,8,128]{2,0,1:T(8,128)(2,1)}), bf16[128,8,128]{2,0,1:T(8,128)(2,1)}, u32[]{:S(2)}, u32[]{:S(2)}) async-start(bf16[128,8,128]{2,0,1:T(8,128)(2,1)} %bitcast.236), calls=%async_computation.5 | async-start | bytes 524288 | tf_op jit(solution)/shard_map/all_to_all | solution.py:226
  697.2 14.3 %all-to-all-start = ((bf16[128,8,128]{2,0,1:T(8,128)(2,1)}), bf16[128,8,128]{2,0,1:T(8,128)(2,1)}, u32[]{:S(2)}, u32[]{:S(2)}) async-start(bf16[128,8,128]{2,0,1:T(8,128)(2,1)} %bitcast.263), calls=%async_computation | async-start | bytes 524288 | tf_op jit(solution)/shard_map/all_to_all | solution.py:224
  711.5 183.8 %all-to-all-start.6 = ((bf16[128,8,512]{2,0,1:T(8,128)(2,1)}), bf16[128,8,512]{2,0,1:T(8,128)(2,1)}, u32[]{:S(2)}, u32[]{:S(2)}) async-start(bf16[128,8,512]{2,0,1:T(8,128)(2,1)} %bitcast.235), calls=%async_computation.6 | async-start | bytes 2097152 | tf_op jit(solution)/shard_map/all_to_all | solution.py:227
  895.3 212.3 %all-to-all-start.7 = ((bf16[128,8,512]{2,0,1:T(8,128)(2,1)}), bf16[128,8,512]{2,0,1:T(8,128)(2,1)S(1)}, u32[]{:S(2)}, u32[]{:S(2)}) async-start(bf16[128,8,512]{2,0,1:T(8,128)(2,1)} %bitcast.234), calls=%async_computation.7 | async-start | bytes 2097152 | tf_op jit(solution)/shard_map/all_to_all | solution.py:227
  1108.6 11.9 all-to-all-start.2
  1120.5 11.8 all-to-all-start.3
  1132.3 11.8 all-to-all-start.1
  1135.7 148.5 %all-reduce.4.cloned.1.call-start = ((), (), s32[]{:S(2)}) async-start(), calls=%async_computation.18 | async-start | bytes 12582912 | tf_op jit(solution)/shard_map/psum | solution.py:241
  1152.7 12.1 all-to-all-start.10
  1164.8 14.8 %all-to-all-start.11 = ((bf16[8,2,256]{2,1,0:T(2,128)(2,1)}), bf16[8,2,256]{2,1,0:T(2,128)(2,1)S(1)}, u32[]{:S(2)}, u32[]{:S(2)}) async-start(bf16[8,2,256]{2,1,0:T(2,128)(2,1)} %reshape.400), calls=%async_computation.11 | async-start | bytes 16384 | tf_op jit(solution)/shard_map/all_to_all | solution.py:30
  1179.6 11.0 all-to-all-start.8
  1190.6 11.0 all-to-all-start.9
  (74 other events, 794.3 us)
Sparse Core Ops, SparseCore 0:
  11.9 189.1 all-gather.10
  203.5 106.7 all-gather.18
  313.2 183.8 all-gather.12
  499.2 106.7 all-gather.20
  665.7 219.1 all-gather.14
  887.6 214.2 all-gather.16
  1148.9 135.2 all-reduce.3
where the time goes:
time: 1310 us; the launch traced here: 1300 us
  waiting for transfers between devices  903 us (69%)
  blocking collectives  148 us (11%)
  matrix products  127 us (10%)
  starting transfers between devices  47.8 us (4%)
  local copies, waits for them, and re-layouts  32.1 us (2%)
  other arithmetic  28.6 us (2%)
  between operations  16 us (1%)
    all_gather x4, waiting for transfers between devices, in_one_piece(): result, at, done = (lax.all_gather(both, axis, axis=dim, tiled=True), 0, [])  611 us
    all_gather x2, waiting for transfers between devices, local(): lax.all_gather(w_down[layer_no], 'shard', axis=0, tiled=True)  185 us
    all_gather x2, blocking collectives, local(): lax.all_gather(up_bias[layer_no], 'shard', axis=0, tiled=True)  59.8 us
    all_gather x2, blocking collectives, in_one_piece(): result, at, done = (lax.all_gather(both, axis, axis=dim, tiled=True), 0, [])  59.5 us
    psum x1, waiting for transfers between devices, local(): lax.psum(shares[0].astype(jnp.bfloat16), 'rep').astype(jnp.float32)  52.5 us
    psum x1, blocking collectives, local(): lax.psum(shares[4].astype(jnp.bfloat16), 'rep').astype(jnp.float32)  28.4 us
  transfers between devices with their start and end apart: 19, of which 16 were waited for; matrix products, arithmetic and copies ran while one was open for 8% of the time, Pallas kernels for 0%

commit v1 on v0

--- a/solution.py
+++ b/solution.py
@@ -1,3 +1,4 @@
+import functools
 import jax
 import jax.numpy as jnp
 from jax import lax
@@ -8,6 +9,21 @@
 LAYERS = 2
 epsilon = 1e-05
 gelu_coef = 0.7978845608
+
+
+def post_the_things(unit, axis_id):
+    return jnp.concatenate(
+        lax.all_to_all(
+            jnp.stack(lax.axis_size(axis_id) * [unit]),
+            axis_name=axis_id,
+            concat_axis=0,
+            split_axis=0,
+        ),
+        axis=0,
+    )
+
+
+supply_series_all = functools.partial(post_the_things, axis_id="shard")
 
 
 def in_one_piece(arrays, axis, dim, along):
@@ -202,7 +218,7 @@
     for layer_no in range(LAYERS):
         whole = (
             *in_one_piece((w_qkv[layer_no], w_proj[layer_no], w_up[layer_no]), "shard", 0, 1),
-            lax.all_gather(w_down[layer_no], "shard", axis=0, tiled=True),
+            supply_series_all(w_down[layer_no]),
             *in_one_piece((norm_gain[layer_no], d_bias[layer_no]), "shard", 0, 1),
             lax.all_gather(up_bias[layer_no], "shard", axis=0, tiled=True),
         )

time: 1310 us -> 1460 us (1.11)
  blocking collectives: 148 us -> 304 us
  waiting for transfers between devices: 903 us -> 876 us
    all_gather x2, blocking collectives: 59.8 us -> 197 us  [local(): lax.all_gather(up_bias[layer_no], 'shard', axis=0, tiled=True)]
    all_gather x4, waiting for transfers between devices: 611 us -> 568 us  [in_one_piece(): result, at, done = (lax.all_gather(both, axis, axis=dim, tiled=True), 0, [])]
    all_to_all x2 -> x1, waiting for transfers between devices: 0.01 us -> 23 us  [local(): lax.all_to_all(kept[12], 'shard', split_axis=1, concat_axis=0, tiled=True)]
    all_to_all x0 -> x1, blocking collectives: none -> 19.5 us  [local(): lax.all_to_all(kept[12], 'shard', split_axis=1, concat_axis=0, tiled=True)]
    all_gather x2, waiting for transfers between devices: 185 us -> 166 us  [local(): lax.all_gather(w_down[layer_no], 'shard', axis=0, tiled=True)]
  transfers between devices with their start and end apart: 19 -> 20, of which waited for: 16 -> 17; matrix products, arithmetic and copies ran while one was open for 8% -> 10% of each run, Pallas kernels for 0% -> 0%
where the time goes in v1:
time: 1460 us
  waiting for transfers between devices  876 us (60%)
  blocking collectives  304 us (21%)
  matrix products  128 us (9%)
  starting transfers between devices  58.5 us (4%)
  local copies, waits for them, and re-layouts  42.4 us (3%)
  other arithmetic  30.3 us (2%)
  between operations  15.7 us (1%)
    all_gather x4, waiting for transfers between devices, in_one_piece(): result, at, done = (lax.all_gather(both, axis, axis=dim, tiled=True), 0, [])  568 us
    all_gather x2, blocking collectives, local(): lax.all_gather(up_bias[layer_no], 'shard', axis=0, tiled=True)  197 us
    all_gather x2, waiting for transfers between devices, local(): lax.all_gather(w_down[layer_no], 'shard', axis=0, tiled=True)  166 us
    all_gather x2, blocking collectives, in_one_piece(): result, at, done = (lax.all_gather(both, axis, axis=dim, tiled=True), 0, [])  59.6 us
    psum x1, waiting for transfers between devices, local(): lax.psum(shares[0].astype(jnp.bfloat16), 'rep').astype(jnp.float32)  52.9 us
  transfers between devices with their start and end apart: 20, of which 17 were waited for; matrix products, arithmetic and copies ran while one was open for 10% of the time, Pallas kernels for 0%

profile of v1, /device:TPU:0, one launch (start us, length us, event | category | flops | bytes accessed | tf_op | source)
XLA Modules:
  0.0 1455.1 jit_solution(18174794522141802623)
XLA Ops:
  29.1 167.1 %all-gather = bf16[1,4096]{1,0:T(2,128)(2,1)S(1)} all-gather(bf16[1,512]{1,0:T(2,128)(2,1)S(1)} %get-tuple-element.109), channel_id=2, replica_groups=mesh['rep'=16,'shard'=8] {'shard'}, dimensions={1}, use_global_device_ids=true | all-gather | bytes 9216 | tf_op jit(solution)/shard_map/all_gather | solution.py:223
  196.2 29.8 %all-gather.1 = bf16[1,4096]{1,0:T(2,128)(2,1)S(1)} all-gather(bf16[1,512]{1,0:T(2,128)(2,1)S(1)} %get-tuple-element.108), channel_id=3, replica_groups=mesh['rep'=16,'shard'=8] {'shard'}, dimensions={1}, use_global_device_ids=true | all-gather | bytes 9216 | tf_op jit(solution)/shard_map/all_gather | solution.py:223
  226.1 29.7 %all_gather.34 = bf16[1024,8]{0,1:T(8,128)(2,1)S(1)} all-gather(bf16[128,8]{0,1:T(8,128)(2,1)S(1)} %pad_maximum_fusion.2), channel_id=1, replica_groups=mesh['rep'=16,'shard'=8] {'shard'}, dimensions={0}, use_global_device_ids=true | all-gather | bytes 18432 | tf_op jit(solution)/shard_map/all_gather | solution.py:31
  255.8 29.9 %all_gather.37 = bf16[1024,8]{0,1:T(8,128)(2,1)S(1)} all-gather(bf16[128,8]{0,1:T(8,128)(2,1)S(1)} %pad_maximum_fusion.3), channel_id=1, replica_groups=mesh['rep'=16,'shard'=8] {'shard'}, dimensions={0}, use_global_device_ids=true | all-gather | bytes 18432 | tf_op jit(solution)/shard_map/all_gather | solution.py:31
  287.0 16.7 %all-gather.11.cloned.1.call-done = bf16[1024,8192]{1,0:T(8,128)(2,1)} async-done(((bf16[128,8192]{1,0:T(8,128)(2,1)}), bf16[1024,8192]{1,0:T(8,128)(2,1)}) %all-gather.11.cloned.1.call-update) | async-done | bytes 16777232 | tf_op jit(solution)/shard_map/all_gather | solution.py:31
  311.6 8.0 multiply_convert_fusion.1
  324.9 165.0 %all-gather.13.cloned.1.call-done = bf16[1024,8192]{1,0:T(8,128)(2,1)} async-done(((bf16[128,8192]{1,0:T(8,128)(2,1)}), bf16[1024,8192]{1,0:T(8,128)(2,1)}) %all-gather.13.cloned.1.call-update) | async-done | bytes 16777232 | tf_op jit(solution)/shard_map/all_gather | solution.py:31
  499.6 7.8 multiply_convert_fusion
  507.4 91.7 %all-gather.19.cloned.1.call-done = bf16[1,4096,1024]{2,1,0:T(8,128)(2,1)} async-done(((bf16[1,512,1024]{2,1,0:T(8,128)(2,1)}), bf16[1,4096,1024]{2,1,0:T(8,128)(2,1)}) %all-gather.19.cloned.1.call-update) | async-done | bytes 8388624 | tf_op jit(solution)/shard_map/all_gather | solution.py:232
  599.1 8.7 convert_dynamic-update-slice_fusion.1
  607.9 7.8 fusion.8
  634.0 74.1 %all-gather.21.cloned.1.call-done = bf16[1,4096,1024]{2,1,0:T(8,128)(2,1)} async-done(((bf16[1,512,1024]{2,1,0:T(8,128)(2,1)}), bf16[1,4096,1024]{2,1,0:T(8,128)(2,1)}) %all-gather.21.cloned.1.call-update) | async-done | bytes 8388624 | tf_op jit(solution)/shard_map/all_gather | solution.py:232
  708.1 8.4 convert_dynamic-update-slice_fusion
  716.6 7.4 fusion.12
  751.0 7.8 all-to-all-done.6
  763.0 9.3 all-to-all-done.7
  777.7 9.1 all-to-all-done.4
  819.1 8.7 all-to-all-done.3
  833.3 23.0 %all-to-all-done.8 = bf16[128,8,512]{2,0,1:T(8,128)(2,1)} async-done(((bf16[128,8,512]{2,0,1:T(8,128)(2,1)}), bf16[128,8,512]{2,0,1:T(8,128)(2,1)}, u32[]{:S(2)}, u32[]{:S(2)}) %all-to-all-start.8) | async-done | bytes 1048608 | tf_op jit(solution)/shard_map/all_to_all | solution.py:243
  856.4 19.5 %all_to_all.178 = bf16[128,8,512]{2,0,1:T(8,128)(2,1)} all-to-all(bf16[128,8,512]{2,0,1:T(8,128)(2,1)} %bitcast.239), channel_id=1, replica_groups=mesh['rep'=16,'shard'=8] {'shard'}, dimensions={1} | all-to-all | bytes 2097152 | tf_op jit(solution)/shard_map/all_to_all | solution.py:243
  885.5 183.6 %all-gather.15.cloned.1.call-done = bf16[1024,9216]{1,0:T(8,128)(2,1)} async-done(((bf16[128,9216]{1,0:T(8,128)(2,1)}), bf16[1024,9216]{1,0:T(8,128)(2,1)}) %all-gather.15.cloned.1.call-update) | async-done | bytes 18874384 | tf_op jit(solution)/shard_map/all_gather | solution.py:31
  1071.8 203.1 %all-gather.17.cloned.1.call-done = bf16[1024,9216]{1,0:T(8,128)(2,1)} async-done(((bf16[128,9216]{1,0:T(8,128)(2,1)}), bf16[1024,9216]{1,0:T(8,128)(2,1)}) %all-gather.17.cloned.1.call-update) | async-done | bytes 18874384 | tf_op jit(solution)/shard_map/all_gather | solution.py:31
  1355.2 28.3 %all-reduce = (bf16[1,128,2]{1,2,0:T(2,128)(2,1)S(1)}, bf16[1,128,2]{1,2,0:T(2,128)(2,1)S(1)}, bf16[1,128,6]{1,2,0:T(8,128)(2,1)S(1)}, bf16[1,128,6]{1,2,0:T(8,1...) all-reduce(bf16[1,128,2]{1,2,0:T(2,128)(2,1)S(1)} %slice_bitcast_fu, ...), channel_id=1, replica_groups=mesh['rep'=16,'shard'=8] {'rep'}, use_global_device_ids=true, to_apply=%region_49.50 | all-reduce | flops 3072 | bytes 12288 | tf_op jit(solution)/shard_map/psum | solution.py:261
  1385.2 52.9 %all-reduce.4.cloned.1.call-done = (bf16[1,128,3072]{2,1,0:T(8,128)(2,1)}, bf16[1,128,3072]{2,1,0:T(8,128)(2,1)}, bf16[1,128,1024]{2,1,0:T(8,128)(2,1)}, bf16[1,...) async-done(((bf16[1,128,3072]{2,1,0:T(8,128)(2,1)}, ...) | async-done | bytes 6291472 | tf_op jit(solution)/shard_map/psum | solution.py:257
  (376 shorter events, 242.1 us)
Async XLA Ops:
  7.2 296.5 %all-gather.11.cloned.1.call-start = ((), (), s32[]{:S(2)}) async-start(), calls=%async_computation.14 | async-start | bytes 18874368 | tf_op jit(solution)/shard_map/all_gather | solution.py:31
  11.8 478.2 %all-gather.13.cloned.1.call-start = ((), (), s32[]{:S(2)}) async-start(), calls=%async_computation.15 | async-start | bytes 18874368 | tf_op jit(solution)/shard_map/all_gather | solution.py:31
  13.3 585.8 %all-gather.19.cloned.1.call-start = ((), (), s32[]{:S(2)}) async-start(), calls=%async_computation.18 | async-start | bytes 9437184 | tf_op jit(solution)/shard_map/all_gather | solution.py:232
  21.2 204.9 %copy-start.79 = (bf16[2,128,2]{1,2,0:T(2,128)(2,1)S(1)}, bf16[2,128,2]{1,2,0:T(2,128)(2,1)}, u32[]{:S(2)}) copy-start(bf16[2,128,2]{1,2,0:T(2,128)(2,1)} %param.17) | copy-start | bytes 3076
  21.2 298.4 %all-to-all-start = ((bf16[8,512,1024]{2,1,0:T(8,128)(2,1)}), bf16[8,512,1024]{2,1,0:T(8,128)(2,1)}, u32[]{:S(2)}, u32[]{:S(2)}) async-start(bf16[8,512,1024]{2,1,0:T(8,128)(2,1)} %stack.156), calls=%async_computation | async-start | bytes 16777216 | tf_op jit(solution)/shard_map/all_to_all | solution.py:16
  28.3 257.7 %copy-start.74 = (s32[128]{0:T(128)S(1)}, s32[128]{0:T(128)}, u32[]{:S(2)}) copy-start(s32[128]{0:T(128)} %param.11) | copy-start | bytes 1540
  28.4 257.9 %copy-start.23 = (f32[128,1024]{1,0:T(8,128)S(1)}, f32[128,1024]{1,0:T(8,128)}, u32[]{:S(2)}) copy-start(f32[128,1024]{1,0:T(8,128)} %param.12) | copy-start | bytes 1572868
  28.4 679.8 %all-gather.21.cloned.1.call-start = ((), (), s32[]{:S(2)}) async-start(), calls=%async_computation.19 | async-start | bytes 9437184 | tf_op jit(solution)/shard_map/all_gather | solution.py:232
  28.9 1040.1 %all-gather.15.cloned.1.call-start = ((), (), s32[]{:S(2)}) async-start(), calls=%async_computation.16 | async-start | bytes 21233664 | tf_op jit(solution)/shard_map/all_gather | solution.py:31
  742.5 532.4 %all-gather.17.cloned.1.call-start = ((), (), s32[]{:S(2)}) async-start(), calls=%async_computation.17 | async-start | bytes 21233664 | tf_op jit(solution)/shard_map/all_gather | solution.py:31
  746.8 11.9 all-to-all-start.6
  758.7 13.5 all-to-all-start.7
  772.2 14.5 all-to-all-start.4
  786.8 14.2 all-to-all-start.5
  801.0 12.9 all-to-all-start.2
  813.9 13.9 all-to-all-start.3
  827.8 28.6 %all-to-all-start.8 = ((bf16[128,8,512]{2,0,1:T(8,128)(2,1)}), bf16[128,8,512]{2,0,1:T(8,128)(2,1)}, u32[]{:S(2)}, u32[]{:S(2)}) async-start(bf16[128,8,512]{2,0,1:T(8,128)(2,1)} %bitcast.238), calls=%async_computation.8 | async-start | bytes 2097152 | tf_op jit(solution)/shard_map/all_to_all | solution.py:243
  880.3 426.2 %all-to-all-start.1 = ((bf16[8,512,1024]{2,1,0:T(8,128)(2,1)}), bf16[8,512,1024]{2,1,0:T(8,128)(2,1)}, u32[]{:S(2)}, u32[]{:S(2)}) async-start(bf16[8,512,1024]{2,1,0:T(8,128)(2,1)} %stack.157), calls=%async_computation.1 | async-start | bytes 16777216 | tf_op jit(solution)/shard_map/all_to_all | solution.py:16
  885.2 389.7 %copy-start.35 = (bf16[128,8,128]{2,0,1:T(8,128)(2,1)S(1)}, bf16[128,8,128]{2,0,1:T(8,128)(2,1)}, u32[]{:S(2)}) copy-start(bf16[128,8,128]{2,0,1:T(8,128)(2,1)} %copy-done.34) | copy-start | bytes 786436
  885.2 552.9 %all-reduce.4.cloned.1.call-start = ((), (), s32[]{:S(2)}) async-start(), calls=%async_computation.20 | async-start | bytes 12582912 | tf_op jit(solution)/shard_map/psum | solution.py:257
  1306.4 12.0 all-to-all-start.12
  1318.4 14.8 %all-to-all-start.13 = ((bf16[8,2,256]{2,1,0:T(2,128)(2,1)}), bf16[8,2,256]{2,1,0:T(2,128)(2,1)S(1)}, u32[]{:S(2)}, u32[]{:S(2)}) async-start(bf16[8,2,256]{2,1,0:T(2,128)(2,1)} %reshape.410), calls=%async_computation.13 | async-start | bytes 16384 | tf_op jit(solution)/shard_map/all_to_all | solution.py:46
  1333.2 11.0 all-to-all-start.10
  1344.1 11.0 all-to-all-start.11
  (77 other events, 1526.8 us)
Sparse Core Ops, SparseCore 0:
  11.9 291.7 all-gather.10
  306.0 183.8 all-gather.12
  492.3 106.7 all-gather.18
  601.3 106.7 all-gather.20
  742.6 326.3 all-gather.14
  1071.8 203.0 all-gather.16
  1302.5 135.5 all-reduce.3
